TPU v7x, 32 devices: a whole 2x2x4 slice. The times are simulated.
32 devices in a mesh: groups: 2 (over y), expo: 4 (over z), tile: 4 (over x, core).
Axes of the slice: x: 2, y: 2, z: 4, core: 2. Of those that a mesh axis runs over, the one named last changes fastest.
Arguments:
- template: bfloat16 [8, 64, 4096], P(('groups', 'expo'), 'tile'), parts along dimension 0
- science: bfloat16 [8, 1, 64, 4096], P(('groups', 'expo'), None, 'tile'), parts along dimension 0
- plan: int32 [8], P('groups'), parts along dimension 0, may hold values from 0 to 3, as said below
- orders: int32 [6, 2], replicated, may hold values from 0 to 2
- coadd_weight: float32 [8, 1], P(('groups', 'expo')), parts along dimension 0, may hold values from 0.3 to 3
- intersection: int32 [8, 1], P(('groups', 'expo')), parts along dimension 0, may hold values 0 or 1
Outputs:
- coadd: float32 [2, 64, 4096], P('groups', 'tile', 'expo'), parts along dimension 0
- coeffs: float32 [8, 1, 13], P(('groups', 'expo')), parts along dimension 0
There are 2 independent parts, one for each index of `groups`. A program takes and returns all parts, laid end to end along the dimension named above; an argument that names none is the same for every part. Nothing has to cross between parts.
Inputs may be any that keep to these rules, and one draw needn't show every extreme that they name: `plan`: a permutation of the group's patch indices.
All inputs are finite; a program needn't handle non-finite values. No bound on the sum of `intersection` on one device may be relied on, other than what follows from the above.
Results may differ from a plain program's by a relative error of at most 0.0061.
Values may be sent and summed in bfloat16 or wider, within the bound.
A program may use at most 64 MiB of HBM per device.

v0:
```python
import jax
import jax.numpy as jnp
from jax import lax
from jax.sharding import PartitionSpec as P

HALF = 15
NB = 6
NU = 13
SIGMAS = (0.8, 1.4, 2.2, 3.0, 4.0, 5.5)
RIDGE = 0.05


def broadcast(block, axis, holder):
    block = jnp.where(lax.axis_index(axis) == holder, block, jnp.zeros_like(block))
    return lax.psum(block, axis)


def extended(x, sides, width):
    for axis, dim in sides:
        size, length = (lax.axis_size(axis), x.shape[dim])
        up = [(i, (i + 1) % size) for i in range(size - 1)]
        down = [(j, i) for i, j in up]
        last = lax.slice_in_dim(x, length - width, length, axis=dim)
        first = lax.slice_in_dim(x, 0, width, axis=dim)
        before = lax.ppermute(last, axis, up)
        after = lax.ppermute(first, axis, down)
        x = jnp.concatenate([before, x, after], axis=dim)
    return x


def make_filters(orders):
    taps_pos = jnp.arange(2 * HALF + 1).astype(jnp.float32) - HALF
    row_list = []
    col_list = []
    for basis in range(NB):
        sigma = SIGMAS[basis]
        envelope = jnp.exp(-taps_pos * taps_pos / (2.0 * sigma * sigma))

        def power(order):
            return jnp.where(order == 0, 1.0, jnp.where(order == 1, taps_pos, taps_pos * taps_pos))

        row_filter = envelope * power(orders[basis, 0])
        col_filter = envelope * power(orders[basis, 1])
        row_list.append(row_filter / jnp.sqrt(jnp.sum(row_filter * row_filter)))
        col_list.append(col_filter / jnp.sqrt(jnp.sum(col_filter * col_filter)))
    return (jnp.stack(row_list).astype(jnp.bfloat16), jnp.stack(col_list).astype(jnp.bfloat16))


def band_matrix(filters, out_len, in_len):
    offset = jnp.arange(in_len)[None, :] - jnp.arange(out_len)[:, None]
    taps_idx = jnp.arange(2 * HALF + 1)
    picks = (offset[:, :, None] == taps_idx[None, None, :]).astype(jnp.float32)
    band = jnp.einsum("ijt,kt->kij", picks, filters.astype(jnp.float32))
    return band.astype(jnp.bfloat16)


def per_device(template, science, plan, orders, coadd_weight, intersection):
    row_filters, col_filters = make_filters(orders)
    rows = template.shape[1]
    width = template.shape[2]
    blocks_count = width // 128
    steps_count = science.shape[1]
    row_band = band_matrix(row_filters, rows, rows + 2 * HALF)
    col_band = jnp.transpose(band_matrix(col_filters, 128, 128 + 2 * HALF), (0, 2, 1))
    column_pos = 2.0 * (jnp.arange(width).astype(jnp.float32) + 0.5) / width - 1.0
    pieces = []
    fitted = []
    for step in range(steps_count):
        owner_index = plan[step]
        received = broadcast(template[0], "expo", owner_index)
        padded = extended(received, (("tile", 0),), HALF)
        rowconv = jnp.einsum(
            "kij,jw->kiw", row_band, padded, preferred_element_type=jnp.float32
        ).astype(jnp.bfloat16)
        blocks = rowconv.reshape(NB, rows, blocks_count, 128)
        empty_rim = jnp.zeros((NB, rows, 1, HALF), jnp.bfloat16)
        previous = jnp.concatenate([empty_rim, blocks[:, :, :-1, 128 - HALF :]], axis=2)
        following = jnp.concatenate([blocks[:, :, 1:, :HALF], empty_rim], axis=2)
        window = jnp.concatenate([previous, blocks, following], axis=3)
        conv = jnp.einsum("krbj,kjc->krbc", window, col_band, preferred_element_type=jnp.float32)
        conv = conv.reshape(NB, rows, width)
        fields = jnp.concatenate(
            [conv, conv * column_pos, jnp.ones((1, rows, width), jnp.float32)], axis=0
        )
        fields = fields.reshape(NU, rows * width)
        exposure_image = science[0, step].astype(jnp.float32).reshape(rows * width)
        normal_local = jnp.dot(fields, fields.T, precision=lax.Precision.HIGHEST)
        project_local = jnp.dot(fields, exposure_image, precision=lax.Precision.HIGHEST)
        normal_matrix, projections = lax.psum((normal_local, project_local), "tile")
        normal_matrix = normal_matrix + RIDGE * (jnp.trace(normal_matrix) / NU) * jnp.eye(
            NU, dtype=jnp.float32
        )
        factor = jnp.linalg.cholesky(normal_matrix)
        coeffs = jax.scipy.linalg.cho_solve((factor, True), projections)
        model = jnp.dot(coeffs, fields, precision=lax.Precision.HIGHEST)
        difference = exposure_image - model
        weight_now = coadd_weight[0, step] * intersection[0, step].astype(jnp.float32)
        pieces.append((weight_now * difference).reshape(rows, width))
        fitted.append(coeffs)
    weighted = jnp.stack(pieces)
    received_parts = lax.all_to_all(weighted[None], "expo", split_axis=3, concat_axis=0, tiled=True)
    coadd = jnp.sum(received_parts, axis=0)
    return (coadd, jnp.stack(fitted)[None])


def solution(mesh):
    return jax.shard_map(
        per_device,
        mesh=mesh,
        in_specs=(
            P(("groups", "expo"), "tile", None),
            P(("groups", "expo"), None, "tile", None),
            P("groups"),
            P(),
            P(("groups", "expo"), None),
            P(("groups", "expo"), None),
        ),
        out_specs=(P("groups", "tile", "expo"), P(("groups", "expo"), None, None)),
        check_vma=False,
    )
```

profile of v0, /device:TPU:0, one launch (start us, length us, event | category | flops | bytes accessed | tf_op | source)
XLA Modules:
  0.0 144.0 jit_solution(105199897231821041)
XLA Ops:
  7.2 0.0 all-reduce.5.cloned.1.call-start
  7.9 0.7 select_bitcast_fusion
  8.5 0.0 all-reduce.5.cloned.1.call-update
  8.6 1.8 %fusion.124 = (s32[1,1]{0,1:T(1,128)}, s32[1,1]{0,1:T(1,128)}, s32[1,1]{0,1:T(1,128)}, s32[1,1]{0,1:T(1,128)}, s32[1,1]{0,1:T(1,128)}, /*index=5*/s32[1,1]{0,1:T...) fusion(s32[6,2]{0,1:T(2,128)} %param.9), kind=kLoop, calls=%fused_computation.211 | loop fusion | bytes 96 | tf_op jit(solution)/shard_map/slice | solution.py:43
  25.6 0.6 fusion.93
  26.9 0.6 fusion.113
  28.2 0.6 fusion.111
  29.5 0.6 fusion.109
  30.8 0.6 fusion.107
  32.1 0.6 fusion.105
  33.4 0.6 fusion.103
  34.7 0.6 fusion.101
  36.1 0.6 fusion.99
  37.4 0.6 fusion.97
  38.7 0.6 fusion.95
  40.0 0.6 fusion.91
  41.5 0.2 convolution_convert_fusion.1
  42.9 1.8 %copy.41 = bf16[1,1,16,4096]{3,1,2,0:T(2,128)(2,1)} copy(bf16[1,1,16,4096]{3,2,1,0:T(8,128)(2,1)} %param.7) | data formatting | bytes 262144
  44.8 0.9 copy.38
  45.7 0.1 copy.40
  45.8 0.6 pad.7.clone
  46.4 1.4 all-reduce.5.cloned.1.call-done
  47.8 1.0 fusion.123
  48.8 1.3 collective-permute-start
  50.1 1.3 collective-permute-start.1
  51.4 0.5 fusion.21
  51.9 0.0 collective-permute-done
  52.0 3.2 %collective-permute-done.1 = bf16[15,4096]{1,0:T(8,128)(2,1)S(1)} collective-permute-done((bf16[15,4096]{1,0:T(8,128)(2,1)S(1)}, bf16[15,4096]{1,0:T(8,128)(2,1)S(1)}, u32[]{:S(2)}, u32[]{:S(2)}) %collective-permute-start.1) | collective-permute-done | bytes 122912 | tf_op jit(solution)/shard_map/ppermute | solution.py:26
  55.2 1.3 convolution_convert_fusion
  56.5 0.2 copy.37
  56.6 0.6 fusion.122
  57.2 1.5 %fusion.10 = f32[6,16,32,128]{3,2,1,0:T(8,128)S(1)} fusion(bf16[6,16,31,15]{3,2,1,0:T(8,128)(2,1)S(1)} %get-tuple-element.9, bf16[6,16,31,15]{3,2,1,0:T(8,128)(2,1)S(1)} %get-tuple-element.8, bf16[6,16,32,128]{3,2,1,0:T(8,128)(2,1)S(1)} %bitcast.105, bf16[6,128,158,1]{1,0,2,3:T(8,128)(2,1)S(1)} %fusion.21), kind=kOutput, calls=%fused_computation.17 | convolution fusion | flops 129110016 | bytes 2780544 | tf_op jit(solution)/shard_map/krbj,kjc->krbc/dot_general | solution.py:80
  58.7 0.3 reshape.337
  59.0 0.0 copy-start.4
  59.0 0.1 broadcast_multiply_fusion.1
  59.2 0.5 copy-done.4
  59.7 0.4 maximum_maximum_fusion.1
  60.1 6.5 %fusion.22 = f32[13,13]{1,0:T(8,128)S(1)} fusion(f32[13,16,4096]{2,1,0:T(8,128)S(1)} %maximum_maximum_fusion.1), kind=kOutput, calls=%fused_computation.28 | convolution fusion | flops 132907008 | bytes 3408548 | tf_op jit(solution)/shard_map/dot_general | solution.py:87
  66.6 1.0 copy.53
  67.6 0.0 copy-start
  67.6 1.0 broadcast_multiply_fusion
  68.6 0.3 copy-done
  68.9 1.0 copy-done.1
  69.9 3.3 %fusion.25 = f32[13]{0:T(128)S(1)} fusion(bf16[65536,1]{0,1:T(2,128)(2,1)S(1)} %bitcast.112, f32[6,65536]{1,0:T(8,128)S(1)} %broadcast_multiply_fusion, f32[6,65536]{1,0:T(8,128)S(1)} %bitcast.100, f32[13]{0:T(128)S(1)} %copy-done.4), kind=kOutput, calls=%fused_computation.30 | convolution fusion | flops 11927552 | bytes 3276904 | tf_op jit(solution)/shard_map/dot_general | solution.py:88
  73.2 9.7 %all-reduce.2 = (f32[13,13]{1,0:T(8,128)S(1)}, f32[13]{0:T(128)S(1)}) all-reduce(f32[13,13]{1,0:T(8,128)S(1)} %fusion.22, f32[13]{0:T(128)S(1)} %fusion.25), channel_id=1, replica_groups=mesh['groups'=2,'expo'=4,'tile'=4] {'tile'}, use_global_device_ids=true, to_apply=%region_13.14 | all-reduce | flops 182 | bytes 1456 | tf_op jit(solution)/shard_map/psum | solution.py:89
  82.9 0.6 select_reduce_fusion.1
  84.2 0.1 copy.31
  84.3 1.2 cholesky.17
  85.5 0.6 compare_reduce_fusion
  86.1 0.6 fusion.34
  86.8 1.0 custom-call.10
  87.8 0.1 convolution_bitcast_fusion
  87.9 0.1 fusion.35
  88.1 5.0 %fusion.2 = f32[1,65536]{1,0:T(1,128)S(1)} fusion(f32[6,65536]{1,0:T(8,128)} %copy-done.1, f32[6,65536]{1,0:T(8,128)} %bitcast.101, f32[13]{0:T(128)S(1)} %copy-done.5, f32[1,13]{1,0:T(1,128)S(1)} %fusion.35), kind=kOutput, calls=%fused_computation.5 | convolution fusion | flops 11927552 | bytes 3407976 | tf_op jit(solution)/shard_map/dot_general | solution.py:95
  93.2 0.1 broadcast_in_dim_stack_reshape.3
  93.2 2.5 %copy.32 = f32[1,1,16,4096]{2,1,0,3:T(1,128)S(1)} copy(f32[1,1,16,4096]{3,2,1,0:T(8,128)S(1)} %broadcast_in_dim_stack_reshape.3) | data formatting | bytes 524288 | tf_op jit(solution)/shard_map/broadcast_in_dim;stack;reshape | solution.py:101
  95.7 0.5 broadcast.809
  96.2 19.4 %reduce.10 = f32[4096,16]{1,0:T(8,128)} reduce(f32[4096,1,1,16]{3,2,1,0:T(1,128)S(1)} %bitcast.102, f32[]{:T(128)} %broadcast.809), dimensions={1,2}, to_apply=%bitcast.92.reduce_sub_computation | reduce | bytes 524292
  115.6 2.3 %reshape.354 = f32[4,1,16384]{2,1,0:T(1,128)S(1)} reshape(f32[4096,16]{1,0:T(8,128)} %reduce.10) | data formatting | bytes 524288
  117.9 13.2 %all_to_all.12 = f32[4,1,16384]{2,1,0:T(1,128)S(1)} all-to-all(f32[4,1,16384]{2,1,0:T(1,128)S(1)} %reshape.354), channel_id=1, replica_groups=mesh['groups'=2,'expo'=4,'tile'=4] {'expo'}, dimensions={0} | all-to-all | bytes 524288 | tf_op jit(solution)/shard_map/all_to_all | solution.py:101
  131.0 1.4 reduce.11
  132.4 3.7 %reshape.355 = f32[4096,1,1,16]{3,2,1,0:T(1,128)S(1)} reshape(f32[4,16384]{1,0:T(4,128)S(1)} %reduce.11) | data formatting | bytes 524288
  136.1 0.2 reduce_sum.142
  136.3 0.8 copy.33
  (23 shorter events, 0.3 us)
Async XLA Ops:
  7.2 40.6 %all-reduce.5.cloned.1.call-start = ((), (), s32[]{:S(2)}) async-start(), calls=%async_computation.1 | async-start | bytes 262144 | tf_op jit(solution)/shard_map/psum | solution.py:15
  48.8 3.1 %collective-permute-start = (bf16[15,4096]{1,0:T(8,128)(2,1)S(1)}, bf16[15,4096]{1,0:T(8,128)(2,1)S(1)}, u32[]{:S(2)}, u32[]{:S(2)}) collective-permute-start(bf16[15,4096]{1,0:T(8,128)(2,1)S(1)} %get-tuple-element.10), channel_id=1, source_target_pairs={{0,1},{1,2},{2,3},{4,5},{5,6},{6,7},{8,9},{9,10},{10,11},{12,13},{... | collective-permute-start | bytes 368648 | tf_op jit(solution)/shard_map/ppermute | solution.py:25
  50.1 5.1 %collective-permute-start.1 = (bf16[15,4096]{1,0:T(8,128)(2,1)S(1)}, bf16[15,4096]{1,0:T(8,128)(2,1)S(1)}, u32[]{:S(2)}, u32[]{:S(2)}) collective-permute-start(bf16[15,4096]{1,0:T(8,128)(2,1)S(1)} %get-tuple-element.11), channel_id=1, source_target_pairs={{1,0},{2,1},{3,2},{5,4},{6,5},{7,6},{9,8},{10,9},{11,10},{13,12},{... | collective-permute-start | bytes 368648 | tf_op jit(solution)/shard_map/ppermute | solution.py:26
  59.0 0.7 copy-start.4
  67.6 1.3 copy-start
  67.6 2.3 %copy-start.2 = (bf16[1,1,16,4096]{3,1,2,0:T(2,128)(2,1)S(1)}, bf16[1,1,16,4096]{3,1,2,0:T(2,128)(2,1)}, u32[]{:S(2)}) copy-start(bf16[1,1,16,4096]{3,1,2,0:T(2,128)(2,1)} %copy.41) | copy-start | bytes 393220
  68.6 1.4 copy-start.1
  69.9 18.1 %copy-start.5 = (f32[13]{0:T(128)S(1)}, f32[13]{0:T(128)}, u32[]{:S(2)}) copy-start(f32[13]{0:T(128)} %pad.7.clone) | copy-start | bytes 160
  88.1 5.0 %copy-start.3 = (f32[1,13]{1,0:T(1,128)}, f32[1,13]{1,0:T(1,128)S(1)}, u32[]{:S(2)}) copy-start(f32[1,13]{1,0:T(1,128)S(1)} %fusion.35) | copy-start | bytes 160
Sparse Core Ops, SparseCore 0:
  10.3 37.4 all-reduce.4
where the time goes:
time: 145 us; the launch traced here: 144 us
  between operations  40.4 us (28%)
  other arithmetic  34.7 us (24%)
  blocking collectives  22.8 us (16%)
  local copies, waits for them, and re-layouts  20.1 us (14%)
  matrix products  18.6 us (13%)
  waiting for transfers between devices  4.66 us (3%)
  starting transfers between devices  2.63 us (2%)
    unnamed x1, other arithmetic  19.4 us
    all_to_all x1, blocking collectives, per_device(): lax.all_to_all(weighted[None], 'expo', split_axis=3, concat_axis=0, tiled...  13.2 us
    unnamed x22, local copies, waits for them, and re-layouts  13.1 us
    psum x1, blocking collectives, per_device(): normal_matrix, projections = lax.psum((normal_local, project_local), 'tile')  9.66 us
    dot_general x1, matrix products, per_device(): normal_local = jnp.dot(fields, fields.T, precision=lax.Precision.HIGHEST)  6.53 us
    dot_general x1, matrix products, per_device(): model = jnp.dot(coeffs, fields, precision=lax.Precision.HIGHEST)  5.02 us
    reduce_sum x6, other arithmetic, make_filters(): col_list.append(col_filter / jnp.sqrt(jnp.sum(col_filter * col_filter)))  3.69 us
    reduce_sum x6, other arithmetic, make_filters(): row_list.append(row_filter / jnp.sqrt(jnp.sum(row_filter * row_filter)))  3.69 us
  transfers between devices with their start and end apart: 3, of which 2 were waited for; matrix products, arithmetic and copies ran while one was open for 9% of the time, Pallas kernels for 0%

commit v1 on v0

--- a/solution.py
+++ b/solution.py
@@ -98,7 +98,11 @@
         pieces.append((weight_now * difference).reshape(rows, width))
         fitted.append(coeffs)
     weighted = jnp.stack(pieces)
-    received_parts = lax.all_to_all(weighted[None], "expo", split_axis=3, concat_axis=0, tiled=True)
+    block_2 = weighted[None]
+    count = lax.axis_size("expo")
+    parts = jnp.stack(jnp.split(block_2, count, axis=3), axis=0)
+    parts = lax.all_to_all(parts, "expo", split_axis=0, concat_axis=0)
+    received_parts = jnp.concatenate(parts, axis=0)
     coadd = jnp.sum(received_parts, axis=0)
     return (coadd, jnp.stack(fitted)[None])
 

time: 145 us -> 115 us (0.79)
  other arithmetic: 34.7 us -> 14.8 us
  local copies, waits for them, and re-layouts: 20.1 us -> 10.3 us
    unnamed x1 -> x0, other arithmetic: 19.4 us -> none
    unnamed x22 -> x18, local copies, waits for them, and re-layouts: 13.1 us -> 5.83 us
    another operation x2, local copies, waits for them, and re-layouts: 2.53 us -> 0.07 us  [the longest x1 0.05 us: per_device(): block_2 = weighted[None]]
  transfers between devices with their start and end apart: 3 -> 3, of which waited for: 2 -> 2; matrix products, arithmetic and copies ran while one was open for 9% -> 12% of each run, Pallas kernels for 0% -> 0%
where the time goes in v1:
time: 115 us; the launch traced here: 114 us
  between operations  40.6 us (35%)
  blocking collectives  22.8 us (20%)
  matrix products  18.5 us (16%)
  other arithmetic  14.8 us (13%)
  local copies, waits for them, and re-layouts  10.3 us (9%)
  waiting for transfers between devices  4.35 us (4%)
  starting transfers between devices  3.01 us (3%)
    all_to_all x1, blocking collectives, per_device(): parts = lax.all_to_all(parts, 'expo', split_axis=0, concat_axis=0)  13.2 us
    psum x1, blocking collectives, per_device(): normal_matrix, projections = lax.psum((normal_local, project_local), 'tile')  9.66 us
    dot_general x1, matrix products, per_device(): normal_local = jnp.dot(fields, fields.T, precision=lax.Precision.HIGHEST)  6.53 us
    unnamed x18, local copies, waits for them, and re-layouts  5.83 us
    dot_general x1, matrix products, per_device(): model = jnp.dot(coeffs, fields, precision=lax.Precision.HIGHEST)  5.02 us
    reduce_sum x6, other arithmetic, make_filters(): col_list.append(col_filter / jnp.sqrt(jnp.sum(col_filter * col_filter)))  3.69 us
    reduce_sum x6, other arithmetic, make_filters(): row_list.append(row_filter / jnp.sqrt(jnp.sum(row_filter * row_filter)))  3.69 us
    ppermute x1, waiting for transfers between devices, extended(): after = lax.ppermute(first, axis, down)  3.59 us
  transfers between devices with their start and end apart: 3, of which 2 were waited for; matrix products, arithmetic and copies ran while one was open for 12% of the time, Pallas kernels for 0%

profile of v1, /device:TPU:0, one launch (start us, length us, event | category | flops | bytes accessed | tf_op | source)
XLA Modules:
  0.0 114.4 jit_solution(10389166510827092128)
XLA Ops:
  7.2 0.0 all-reduce.5.cloned.1.call-start
  7.9 0.7 select_bitcast_fusion
  8.5 0.0 all-reduce.5.cloned.1.call-update
  8.6 1.8 %fusion.128 = (s32[1,1]{0,1:T(1,128)}, s32[1,1]{0,1:T(1,128)}, s32[1,1]{0,1:T(1,128)}, s32[1,1]{0,1:T(1,128)}, s32[1,1]{0,1:T(1,128)}, /*index=5*/s32[1,1]{0,1:T...) fusion(s32[6,2]{0,1:T(2,128)} %param.9), kind=kLoop, calls=%fused_computation.216 | loop fusion | bytes 96 | tf_op jit(solution)/shard_map/slice | solution.py:43
  27.1 0.6 fusion.97
  28.4 0.6 fusion.117
  29.7 0.6 fusion.115
  31.0 0.6 fusion.113
  32.3 0.6 fusion.111
  33.6 0.6 fusion.109
  34.9 0.6 fusion.107
  36.2 0.6 fusion.105
  37.6 0.6 fusion.103
  38.9 0.6 fusion.101
  40.2 0.6 fusion.99
  41.5 0.6 fusion.95
  42.8 1.8 %copy.27 = bf16[1,1,16,4096]{3,1,2,0:T(2,128)(2,1)} copy(bf16[1,1,16,4096]{3,2,1,0:T(8,128)(2,1)} %param.7) | data formatting | bytes 262144
  44.6 0.9 copy.23
  45.6 0.1 copy.26
  45.6 0.3 iota_compare_fusion.2
  46.0 0.6 pad.11.clone
  46.8 0.2 convolution_convert_fusion.1
  46.9 0.7 all-reduce.5.cloned.1.call-done
  47.7 1.0 fusion.127
  48.7 1.7 %collective-permute-start = (bf16[15,4096]{1,0:T(8,128)(2,1)S(1)}, bf16[15,4096]{1,0:T(8,128)(2,1)S(1)}, u32[]{:S(2)}, u32[]{:S(2)}) collective-permute-start(bf16[15,4096]{1,0:T(8,128)(2,1)S(1)} %get-tuple-element.10), channel_id=1, source_target_pairs={{0,1},{1,2},{2,3},{4,5},{5,6},{6,7},{8,9},{9,10},{10,11},{12,13},{... | collective-permute-start | bytes 368648 | tf_op jit(solution)/shard_map/ppermute | solution.py:25
  50.4 1.3 %collective-permute-start.1 = (bf16[15,4096]{1,0:T(8,128)(2,1)S(1)}, bf16[15,4096]{1,0:T(8,128)(2,1)S(1)}, u32[]{:S(2)}, u32[]{:S(2)}) collective-permute-start(bf16[15,4096]{1,0:T(8,128)(2,1)S(1)} %get-tuple-element.11), channel_id=1, source_target_pairs={{1,0},{2,1},{3,2},{5,4},{6,5},{7,6},{9,8},{10,9},{11,10},{13,12},{... | collective-permute-start | bytes 368648 | tf_op jit(solution)/shard_map/ppermute | solution.py:26
  51.7 0.4 fusion.23
  52.1 0.0 collective-permute-done
  52.1 3.6 %collective-permute-done.1 = bf16[15,4096]{1,0:T(8,128)(2,1)S(1)} collective-permute-done((bf16[15,4096]{1,0:T(8,128)(2,1)S(1)}, bf16[15,4096]{1,0:T(8,128)(2,1)S(1)}, u32[]{:S(2)}, u32[]{:S(2)}) %collective-permute-start.1) | collective-permute-done | bytes 122912 | tf_op jit(solution)/shard_map/ppermute | solution.py:26
  55.7 1.3 %convolution_convert_fusion = bf16[6,16,4096]{2,1,0:T(8,128)(2,1)S(1)} fusion(bf16[15,4096]{1,0:T(8,128)(2,1)S(1)} %collective-permute-done.1, bf16[16,4096]{1,0:T(8,128)(2,1)} %all-reduce.5.cloned.1.call-done, bf16[15,4096]{1,0:T(8,128)(2,1)S(1)} %collective-permute-done, bf16[6,16,46]{2,0,1:T(8,128)(2,1)S(1)} %convolution_convert_fusion.1), kind=kOutput, calls=%fused_computation | convolution fusion | flops 37699584 | bytes 1172096 | tf_op jit(solution)/shard_map/kij,jw->kiw/dot_general | solution.py:72
  57.0 0.2 copy.24
  57.1 0.6 fusion.126
  57.7 1.5 %fusion.11 = f32[6,16,32,128]{3,2,1,0:T(8,128)S(1)} fusion(bf16[6,16,31,15]{3,2,1,0:T(8,128)(2,1)S(1)} %get-tuple-element.5, bf16[6,16,31,15]{3,2,1,0:T(8,128)(2,1)S(1)} %get-tuple-element.4, bf16[6,16,32,128]{3,2,1,0:T(8,128)(2,1)S(1)} %bitcast.108, bf16[6,128,158,1]{1,0,2,3:T(8,128)(2,1)S(1)} %fusion.23), kind=kOutput, calls=%fused_computation.18 | convolution fusion | flops 129110016 | bytes 2780544 | tf_op jit(solution)/shard_map/krbj,kjc->krbc/dot_general | solution.py:80
  59.3 0.3 reshape.337
  59.5 0.0 copy-start.4
  59.6 0.1 broadcast_multiply_fusion.1
  59.7 0.5 copy-done.4
  60.2 0.4 maximum_maximum_fusion.1
  60.6 6.5 %fusion.26 = f32[13,13]{1,0:T(8,128)S(1)} fusion(f32[13,16,4096]{2,1,0:T(8,128)S(1)} %maximum_maximum_fusion.1), kind=kOutput, calls=%fused_computation.28 | convolution fusion | flops 132907008 | bytes 3408548 | tf_op jit(solution)/shard_map/dot_general | solution.py:87
  67.1 1.0 copy.45
  68.1 0.0 copy-start
  68.1 0.0 copy-start.2
  68.1 1.0 broadcast_multiply_fusion
  69.1 0.0 copy-start.1
  69.1 0.3 copy-done
  69.4 1.0 copy-done.1
  70.4 0.0 copy-done.2
  70.4 0.0 copy-start.5
  70.4 3.3 %fusion.29 = f32[13]{0:T(128)S(1)} fusion(bf16[65536,1]{0,1:T(2,128)(2,1)S(1)} %bitcast.114, f32[6,65536]{1,0:T(8,128)S(1)} %broadcast_multiply_fusion, f32[6,65536]{1,0:T(8,128)S(1)} %bitcast.105, f32[13]{0:T(128)S(1)} %copy-done.4), kind=kOutput, calls=%fused_computation.30 | convolution fusion | flops 11927552 | bytes 3276904 | tf_op jit(solution)/shard_map/dot_general | solution.py:88
  73.7 9.7 %all-reduce.2 = (f32[13,13]{1,0:T(8,128)S(1)}, f32[13]{0:T(128)S(1)}) all-reduce(f32[13,13]{1,0:T(8,128)S(1)} %fusion.26, f32[13]{0:T(128)S(1)} %fusion.29), channel_id=1, replica_groups=mesh['groups'=2,'expo'=4,'tile'=4] {'tile'}, use_global_device_ids=true, to_apply=%region_13.14 | all-reduce | flops 182 | bytes 1456 | tf_op jit(solution)/shard_map/psum | solution.py:89
  83.4 0.6 select_reduce_fusion.1
  84.7 0.1 copy.19
  84.8 1.2 %cholesky.17 = f32[13,13]{1,0:T(8,128)S(1)} custom-call(f32[13,13]{1,0:T(8,128)S(1)} %fusion.42), custom_call_target="Cholesky" | custom-call | tf_op jit(solution)/shard_map/jit(cholesky)/cholesky | solution.py:93
  86.0 0.6 compare_reduce_fusion
  86.6 0.6 fusion.38
  87.3 1.0 custom-call.10
  88.3 0.1 convolution_bitcast_fusion
  88.4 0.1 fusion.39
  88.6 0.0 copy-done.5
  88.6 5.0 %fusion.2 = f32[1,65536]{1,0:T(1,128)S(1)} fusion(f32[6,65536]{1,0:T(8,128)} %copy-done.1, f32[6,65536]{1,0:T(8,128)} %bitcast.106, f32[13]{0:T(128)S(1)} %copy-done.5, f32[1,13]{1,0:T(1,128)S(1)} %fusion.39), kind=kOutput, calls=%fused_computation.5 | convolution fusion | flops 11927552 | bytes 3407976 | tf_op jit(solution)/shard_map/dot_general | solution.py:95
  93.7 0.0 copy-done.3
  93.7 0.1 broadcast_in_dim_stack_reshape.3
  93.8 13.2 %all_to_all.5 = f32[4,1,1,16,1024]{4,3,2,1,0:T(8,128)S(1)} all-to-all(f32[4,1,1,16,1024]{4,3,2,1,0:T(8,128)S(1)} %pad_maximum_fusion), channel_id=1, replica_groups=mesh['groups'=2,'expo'=4,'tile'=4] {'expo'}, dimensions={0} | all-to-all | bytes 524288 | tf_op jit(solution)/shard_map/all_to_all | solution.py:104
  106.9 0.6 reduce_sum.142
  (19 shorter events, 0.3 us)
Async XLA Ops:
  7.2 40.5 %all-reduce.5.cloned.1.call-start = ((), (), s32[]{:S(2)}) async-start(), calls=%async_computation.1 | async-start | bytes 262144 | tf_op jit(solution)/shard_map/psum | solution.py:15
  48.7 3.4 %collective-permute-start = (bf16[15,4096]{1,0:T(8,128)(2,1)S(1)}, bf16[15,4096]{1,0:T(8,128)(2,1)S(1)}, u32[]{:S(2)}, u32[]{:S(2)}) collective-permute-start(bf16[15,4096]{1,0:T(8,128)(2,1)S(1)} %get-tuple-element.10), channel_id=1, source_target_pairs={{0,1},{1,2},{2,3},{4,5},{5,6},{6,7},{8,9},{9,10},{10,11},{12,13},{... | collective-permute-start | bytes 368648 | tf_op jit(solution)/shard_map/ppermute | solution.py:25
  50.4 5.3 %collective-permute-start.1 = (bf16[15,4096]{1,0:T(8,128)(2,1)S(1)}, bf16[15,4096]{1,0:T(8,128)(2,1)S(1)}, u32[]{:S(2)}, u32[]{:S(2)}) collective-permute-start(bf16[15,4096]{1,0:T(8,128)(2,1)S(1)} %get-tuple-element.11), channel_id=1, source_target_pairs={{1,0},{2,1},{3,2},{5,4},{6,5},{7,6},{9,8},{10,9},{11,10},{13,12},{... | collective-permute-start | bytes 368648 | tf_op jit(solution)/shard_map/ppermute | solution.py:26
  59.5 0.7 copy-start.4
  68.1 1.3 %copy-start = (f32[1,6,512,128]{3,1,2,0:T(8,128)}, f32[1,6,512,128]{3,1,2,0:T(8,128)S(1)}, u32[]{:S(2)}) copy-start(f32[1,6,512,128]{3,1,2,0:T(8,128)S(1)} %copy.45) | copy-start | bytes 4718596
  68.1 2.3 %copy-start.2 = (bf16[1,1,16,4096]{3,1,2,0:T(2,128)(2,1)S(1)}, bf16[1,1,16,4096]{3,1,2,0:T(2,128)(2,1)}, u32[]{:S(2)}) copy-start(bf16[1,1,16,4096]{3,1,2,0:T(2,128)(2,1)} %copy.27) | copy-start | bytes 393220
  69.1 1.4 %copy-start.1 = (f32[6,65536]{1,0:T(8,128)}, f32[6,65536]{1,0:T(8,128)S(1)}, u32[]{:S(2)}) copy-start(f32[6,65536]{1,0:T(8,128)S(1)} %broadcast_multiply_fusion) | copy-start | bytes 4718596
  70.4 18.1 %copy-start.5 = (f32[13]{0:T(128)S(1)}, f32[13]{0:T(128)}, u32[]{:S(2)}) copy-start(f32[13]{0:T(128)} %pad.11.clone) | copy-start | bytes 160
  88.6 5.1 %copy-start.3 = (f32[1,13]{1,0:T(1,128)}, f32[1,13]{1,0:T(1,128)S(1)}, u32[]{:S(2)}) copy-start(f32[1,13]{1,0:T(1,128)S(1)} %fusion.39) | copy-start | bytes 160
Sparse Core Ops, SparseCore 0:
  10.3 37.3 all-reduce.4
